TPU v7x, 128 devices: a whole 4x4x4 slice. The times are simulated.
128 devices in a mesh: pts: 32 (over z, x, core), rep: 4 (over y).
Axes of the slice: x: 4, y: 4, z: 4, core: 2. Of those that a mesh axis runs over, the one named last changes fastest.
Arguments:
- target_xyz: float32 [3, 32768], P(None, 'pts'), may hold values from 0 to 1
- source_xyz: float32 [3, 65536], P(None, ('pts', 'rep')), may hold values from 0 to 1
- target_count: int32 [32], P('pts'), may hold values from 1 to 1024, as said below
- source_count: int32 [128], P(('pts', 'rep')), may hold values from 1 to 512, as said below
- psi: bfloat16 [32768, 256], P('pts'), may hold values from -6 to 6
- omega: bfloat16 [65536, 256], P(('pts', 'rep')), may hold values from -6 to 6
Outputs:
- range_sketch: float32 [32768, 256], P('pts')
- corange_sketch: float32 [65536, 256], P(('pts', 'rep'))
- core: float32 [256, 256], replicated
- range_gram: float32 [256, 256], replicated
- corange_gram: float32 [256, 256], replicated
Inputs may be any that keep to these rules, and one draw needn't show every extreme that they name: `target_count`: each group holds 1 to 1024 live targets; some group holds exactly 1024. `source_count`: each shard holds 1 to 512 live sources; some shard holds exactly 512.
All inputs are finite; a program needn't handle non-finite values.
Results may differ from a plain program's by a relative error of at most 0.0003.
The roundings to bfloat16 on the way count: a program that leaves them out, or rounds other values in their place, can miss the bound.
Values may be sent and summed in bfloat16 or wider, within the bound.
No kernel may reach another device: no remote copies, remote signals or barrier semaphores. Data moves between devices by JAX's collectives and lax.ppermute only.
A program may use at most 64 MiB of HBM per device.

v0:
```python
import math
import jax
import jax.numpy as jnp
from jax import lax
from jax.sharding import PartitionSpec as P

SHIFT = 1.05
SPREAD = 8.0


def tile_block(tgt, src):
    dx = tgt[0][:, None] - (src[0][None, :] + SHIFT)
    dy = SPREAD * (tgt[1][:, None] - src[1][None, :])
    dz = SPREAD * (tgt[2][:, None] - src[2][None, :])
    return lax.rsqrt(dx * dx + dy * dy + dz * dz).astype(jnp.bfloat16)


def local(target_xyz, source_xyz, target_count, source_count, psi, omega):
    tcap = psi.shape[0]
    scap = omega.shape[0]
    width = psi.shape[1]
    n_pts = lax.axis_size("pts")
    n_rep = lax.axis_size("rep")
    all_targets = tcap * n_pts
    all_sources = scap * n_pts * n_rep
    tlive = jnp.arange(tcap, dtype=jnp.int32) < target_count[0]
    slive = jnp.arange(scap, dtype=jnp.int32) < source_count[0]
    psi_live = jnp.where(tlive[:, None], psi, jnp.zeros_like(psi))
    omega_live = jnp.where(slive[:, None], omega, jnp.zeros_like(omega))
    hi = lax.Precision.HIGHEST
    src_all = lax.all_gather(source_xyz, "pts", axis=1, tiled=True)
    piece = lax.all_gather(omega_live, "pts", axis=0, tiled=True)

    def range_inner(j, acc):
        rows = lax.dynamic_slice_in_dim(piece, j * scap, scap, 0)
        where = lax.dynamic_slice_in_dim(src_all, j * scap, scap, 1)
        return acc + jnp.dot(
            tile_block(target_xyz, where), rows, preferred_element_type=jnp.float32
        )

    y_part = lax.fori_loop(
        0, piece.shape[0] // scap, range_inner, jnp.zeros((tcap, width), jnp.float32)
    )
    y_sum = lax.psum(y_part, "rep") * (2.0 / math.sqrt(all_sources))
    range_sketch = jnp.where(tlive[:, None], y_sum, jnp.zeros_like(y_sum))
    tgt_all = lax.all_gather(target_xyz, "pts", axis=1, tiled=True)
    corange_piece = lax.all_gather(psi_live, "pts", axis=0, tiled=True)

    def corange_inner(j, acc):
        rows = lax.dynamic_slice_in_dim(corange_piece, j * tcap, tcap, 0)
        where = lax.dynamic_slice_in_dim(tgt_all, j * tcap, tcap, 1)
        tile = tile_block(where, source_xyz)
        return acc + lax.dot_general(
            tile, rows, (((0,), (0,)), ((), ())), preferred_element_type=jnp.float32
        )

    z_sum = lax.fori_loop(
        0, corange_piece.shape[0] // tcap, corange_inner, jnp.zeros((scap, width), jnp.float32)
    )
    z_scaled = z_sum * (2.0 / math.sqrt(all_targets))
    corange_sketch = jnp.where(slive[:, None], z_scaled, jnp.zeros_like(z_scaled))
    z_gram_part = jnp.dot(corange_sketch.T, corange_sketch, precision=hi)
    core_part = jnp.dot(psi_live.astype(jnp.float32).T, range_sketch, precision=hi)
    y_gram_part = jnp.dot(range_sketch.T, range_sketch, precision=hi)
    core_sum, y_gram = lax.psum((core_part, y_gram_part), "pts")
    z_gram = lax.psum(z_gram_part, ("pts", "rep"))
    core = core_sum / math.sqrt(all_targets)
    range_gram = y_gram / all_targets
    corange_gram = z_gram / all_sources
    return (range_sketch, corange_sketch, core, range_gram, corange_gram)


def solution(mesh):
    return jax.shard_map(
        local,
        mesh=mesh,
        in_specs=(
            P(None, "pts"),
            P(None, ("pts", "rep")),
            P("pts"),
            P(("pts", "rep")),
            P("pts", None),
            P(("pts", "rep"), None),
        ),
        out_specs=(P("pts", None), P(("pts", "rep"), None), P(), P(), P()),
        check_vma=False,
    )
```

profile of v0, /device:TPU:1, one launch (start us, length us, event | category | flops | bytes accessed | tf_op | source)
XLA Modules:
  0.0 550.0 jit_solution(14603858195827019406)
XLA Ops:
  9.7 27.6 %all_gather.12 = f32[3,16384]{1,0:T(4,128)S(1)} all-gather(f32[3,512]{1,0:T(4,128)} %param.11), channel_id=1, replica_groups=mesh['pts'=32,'rep'=4] {'pts'}, dimensions={1}, use_global_device_ids=true | all-gather | bytes 202752 | tf_op jit(solution)/shard_map/all_gather | solution.py:31
  37.3 30.2 %all-gather.3.cloned.1.call-done = bf16[16384,256]{1,0:T(8,128)(2,1)} async-done(((bf16[512,256]{1,0:T(8,128)(2,1)}), bf16[16384,256]{1,0:T(8,128)(2,1)}) %all-gather.3.cloned.1.call-update) | async-done | bytes 8388624 | tf_op jit(solution)/shard_map/all_gather | solution.py:32
  67.5 96.4 %while.28 = (s32[]{:T(128)}, f32[1024,256]{1,0:T(8,128)S(1)}, f32[3,1024]{1,0:T(4,128)}, f32[3,16384]{1,0:T(4,128)S(1)}, bf16[16384,256]{1,0:T(8,128)(2,1)}, /*i...) while((s32[]{:T(128)}, f32[1024,256]{1,0:T(8,128)S(1)}, ...), condition=%wide.region_1.2_spmd.clone, body=%wide.region_0.1_spmd.clone.sunk | while | flops 274727424 | bytes 2414797 | solution.py:41
  68.4 2.0 convolution_add_fusion.4
  71.4 2.0 convolution_add_fusion.4
  74.5 2.0 convolution_add_fusion.4
  80.5 2.0 convolution_add_fusion.4
  83.5 2.0 convolution_add_fusion.4
  86.5 2.0 convolution_add_fusion.4
  92.5 2.0 convolution_add_fusion.4
  95.5 2.0 convolution_add_fusion.4
  98.6 2.0 convolution_add_fusion.4
  104.6 2.0 convolution_add_fusion.4
  107.6 2.0 convolution_add_fusion.4
  110.6 2.0 convolution_add_fusion.4
  116.6 2.0 convolution_add_fusion.4
  119.6 2.0 convolution_add_fusion.4
  122.7 2.0 convolution_add_fusion.4
  128.7 2.0 convolution_add_fusion.4
  131.7 2.0 convolution_add_fusion.4
  134.7 2.0 convolution_add_fusion.4
  143.7 2.0 convolution_add_fusion.4
  146.8 2.0 convolution_add_fusion.4
  155.8 2.0 convolution_add_fusion.4
  158.8 2.0 convolution_add_fusion.4
  166.7 24.7 %all_gather.14 = f32[3,32768]{1,0:T(4,128)S(1)} all-gather(f32[3,1024]{1,0:T(4,128)S(1)} %copy-done.5), channel_id=1, replica_groups=mesh['pts'=32,'rep'=4] {'pts'}, dimensions={1}, use_global_device_ids=true | all-gather | bytes 405504 | tf_op jit(solution)/shard_map/all_gather | solution.py:46
  191.4 17.0 %all-reduce.5.cloned.1.call-done = f32[1024,256]{1,0:T(8,128)} async-done(((f32[1024,256]{1,0:T(8,128)}), f32[1024,256]{1,0:T(8,128)}) %all-reduce.5.cloned.1.call-update) | async-done | bytes 1048592 | tf_op jit(solution)/shard_map/psum | solution.py:44
  211.4 2.6 fusion.22
  214.0 73.1 %all-gather.5.cloned.1.call-done = bf16[32768,256]{1,0:T(8,128)(2,1)} async-done(((bf16[1024,256]{1,0:T(8,128)(2,1)}), bf16[32768,256]{1,0:T(8,128)(2,1)}) %all-gather.5.cloned.1.call-update) | async-done | bytes 16777232 | tf_op jit(solution)/shard_map/all_gather | solution.py:47
  287.1 81.4 %while.29 = (s32[]{:T(128)}, f32[512,256]{1,0:T(8,128)S(1)}, f32[3,32768]{1,0:T(4,128)S(1)}, f32[3,512]{1,0:T(4,128)S(1)}, bf16[32768,256]{1,0:T(8,128)(2,1)}, /...) while((s32[]{:T(128)}, f32[512,256]{1,0:T(8,128)S(1)}, ...), condition=%wide.region_4.5_spmd.clone, body=%wide.region_3.4_spmd.clone.sunk | while | flops 274465280 | bytes 1628365 | solution.py:57
  287.2 2.4 convolution_add_fusion.5
  289.8 2.4 convolution_add_fusion.5
  292.3 2.4 convolution_add_fusion.5
  294.8 2.4 convolution_add_fusion.5
  297.4 2.4 convolution_add_fusion.5
  300.0 2.4 convolution_add_fusion.5
  302.5 2.4 convolution_add_fusion.5
  305.0 2.4 convolution_add_fusion.5
  307.6 2.4 convolution_add_fusion.5
  310.1 2.4 convolution_add_fusion.5
  312.7 2.4 convolution_add_fusion.5
  315.2 2.4 convolution_add_fusion.5
  317.8 2.4 convolution_add_fusion.5
  320.3 2.4 convolution_add_fusion.5
  322.9 2.4 convolution_add_fusion.5
  325.4 2.4 convolution_add_fusion.5
  327.9 2.4 convolution_add_fusion.5
  330.5 2.4 convolution_add_fusion.5
  333.0 2.4 convolution_add_fusion.5
  335.6 2.4 convolution_add_fusion.5
  338.1 2.4 convolution_add_fusion.5
  340.7 2.4 convolution_add_fusion.5
  343.2 2.4 convolution_add_fusion.5
  345.8 2.4 convolution_add_fusion.5
  348.3 2.4 convolution_add_fusion.5
  350.9 2.4 convolution_add_fusion.5
  353.4 2.4 convolution_add_fusion.5
  355.9 2.4 convolution_add_fusion.5
  358.5 2.4 convolution_add_fusion.5
  361.0 2.4 convolution_add_fusion.5
  363.6 2.4 convolution_add_fusion.5
  366.1 2.4 convolution_add_fusion.5
  370.5 24.1 %all-reduce.9.cloned.1.call-done = (f32[256,256]{1,0:T(8,128)}, f32[256,256]{1,0:T(8,128)}) async-done(((f32[256,256]{1,0:T(8,128)}, f32[256,256]{1,0:T(8,128)}), (f32[256,256]{1,0:T(8,128)}, f32[256,256]{1,0:T(8,128)})) %all-reduce.9.cloned.1.call-update) | async-done | bytes 524304 | tf_op jit(solution)/shard_map/psum | solution.py:65
  396.4 145.4 %all-reduce.7.cloned.1.call-done = f32[256,256]{1,0:T(8,128)} async-done(((f32[256,256]{1,0:T(8,128)}), f32[256,256]{1,0:T(8,128)}) %all-reduce.7.cloned.1.call-update) | async-done | bytes 262160 | tf_op jit(solution)/shard_map/psum | solution.py:66
  (174 shorter events, 65.8 us)
Async XLA Ops:
  7.2 60.3 %all-gather.3.cloned.1.call-start = ((), (), s32[]{:S(2)}) async-start(), calls=%async_computation | async-start | bytes 8650752 | tf_op jit(solution)/shard_map/all_gather | solution.py:32
  9.7 198.7 %all-reduce.5.cloned.1.call-start = ((), (), s32[]{:S(2)}) async-start(), calls=%async_computation.1 | async-start | bytes 2097152 | tf_op jit(solution)/shard_map/psum | solution.py:44
  67.5 98.1 %copy-start.4 = (bf16[1024,256]{1,0:T(8,128)(2,1)S(1)}, bf16[1024,256]{1,0:T(8,128)(2,1)}, u32[]{:S(2)}) copy-start(bf16[1024,256]{1,0:T(8,128)(2,1)} %param.14) | copy-start | bytes 1572868
  163.9 1.0 copy-start.3
  163.9 2.8 copy-start.5
  164.9 122.2 %all-gather.5.cloned.1.call-start = ((), (), s32[]{:S(2)}) async-start(), calls=%async_computation.2 | async-start | bytes 17301504 | tf_op jit(solution)/shard_map/all_gather | solution.py:47
  166.6 43.2 %copy-start.2 = (bf16[1024,256]{1,0:T(8,128)(2,1)S(1)}, bf16[1024,256]{1,0:T(8,128)(2,1)}, u32[]{:S(2)}) copy-start(bf16[1024,256]{1,0:T(8,128)(2,1)} %broadcast_select_fusion) | copy-start | bytes 1572868
  166.6 227.9 %all-reduce.9.cloned.1.call-start = ((), (), s32[]{:S(2)}) async-start(), calls=%async_computation.4 | async-start | bytes 1048576 | tf_op jit(solution)/shard_map/psum | solution.py:65
  209.8 4.1 copy-start
  209.9 77.3 %copy-start.6 = (f32[3,512]{1,0:T(4,128)S(1)}, f32[3,512]{1,0:T(4,128)}, u32[]{:S(2)}) copy-start(f32[3,512]{1,0:T(4,128)} %param.11) | copy-start | bytes 18436
  214.0 327.8 %all-reduce.7.cloned.1.call-start = ((), (), s32[]{:S(2)}) async-start(), calls=%async_computation.3 | async-start | bytes 524288 | tf_op jit(solution)/shard_map/psum | solution.py:66
  368.7 174.8 %copy-start.1 = (f32[512,256]{1,0:T(8,128)}, f32[512,256]{1,0:T(8,128)S(1)}, u32[]{:S(2)}) copy-start(f32[512,256]{1,0:T(8,128)S(1)} %multiply_select_fusion.1) | copy-start | bytes 1572868
Sparse Core Ops, SparseCore 0:
  10.8 56.6 all-gather.2
  165.0 43.3 all-reduce.4
  211.2 75.8 all-gather.4
  290.8 103.6 all-reduce.8
  399.1 142.5 all-reduce.6
where the time goes:
time: 555 us; the launch traced here: 550 us
  waiting for transfers between devices  290 us (52%)
  matrix products  148 us (27%)
  blocking collectives  52.2 us (9%)
  local copies, waits for them, and re-layouts  30.9 us (6%)
  between operations  15.2 us (3%)
  other arithmetic  10.8 us (2%)
    psum x1, waiting for transfers between devices, local(): z_gram = lax.psum(z_gram_part, ('pts', 'rep'))  145 us
    dot_general x32, matrix products, corange_inner(): lax.dot_general(tile, rows, (((0,), (0,)), ((), ())), preferred_element_t...  76.9 us
    all_gather x1, waiting for transfers between devices, local(): corange_piece = lax.all_gather(psi_live, 'pts', axis=0, tiled=True)  73.1 us
    dot_general x32, matrix products, range_inner(): jnp.dot(tile_block(target_xyz, where), rows, preferred_element_type=jnp.f...  65.5 us
    all_gather x1, waiting for transfers between devices, local(): piece = lax.all_gather(omega_live, 'pts', axis=0, tiled=True)  30.2 us
    slice x64, local copies, waits for them, and re-layouts, tile_block(): dx = tgt[0][:, None] - (src[0][None, :] + SHIFT)  30 us
    all_gather x1, blocking collectives, local(): src_all = lax.all_gather(source_xyz, 'pts', axis=1, tiled=True)  27.6 us
    all_gather x1, blocking collectives, local(): tgt_all = lax.all_gather(target_xyz, 'pts', axis=1, tiled=True)  24.7 us
  transfers between devices with their start and end apart: 5, of which 5 were waited for; matrix products, arithmetic and copies ran while one was open for 16% of the time, Pallas kernels for 0%

commit v1 on v0

--- a/solution.py
+++ b/solution.py
@@ -44,7 +44,10 @@
     y_sum = lax.psum(y_part, "rep") * (2.0 / math.sqrt(all_sources))
     range_sketch = jnp.where(tlive[:, None], y_sum, jnp.zeros_like(y_sum))
     tgt_all = lax.all_gather(target_xyz, "pts", axis=1, tiled=True)
-    corange_piece = lax.all_gather(psi_live, "pts", axis=0, tiled=True)
+    n_dev = lax.axis_size("pts")
+    pieces = jnp.stack([psi_live for _ in range(n_dev)])
+    pieces = lax.all_to_all(pieces, "pts", split_axis=0, concat_axis=0)
+    corange_piece = jnp.concatenate(pieces, axis=0)
 
     def corange_inner(j, acc):
         rows = lax.dynamic_slice_in_dim(corange_piece, j * tcap, tcap, 0)

time: 555 us -> 710 us (1.28)
  blocking collectives: 52.2 us -> 270 us
  waiting for transfers between devices: 290 us -> 240 us
  local copies, waits for them, and re-layouts: 30.9 us -> 10.2 us
  starting transfers between devices: 0.21 us -> 9.77 us
    all_gather x1, blocking collectives: 27.6 us -> 244 us  [local(): src_all = lax.all_gather(source_xyz, 'pts', axis=1, tiled=True)]
    psum x1, waiting for transfers between devices: 24.1 us -> 104 us  [local(): core_sum, y_gram = lax.psum((core_part, y_gram_part), 'pts')]
    all_gather x1 -> x0, waiting for transfers between devices: 73.1 us -> none  [local(): corange_piece = lax.all_gather(psi_live, 'pts', axis=0, tiled=True)]
    all_gather x1, waiting for transfers between devices: 30.2 us -> 0.01 us  [local(): piece = lax.all_gather(omega_live, 'pts', axis=0, tiled=True)]
    slice x64, local copies, waits for them, and re-layouts: 30 us -> 3.26 us  [tile_block(): dx = tgt[0][:, None] - (src[0][None, :] + SHIFT)]
    psum x1, waiting for transfers between devices: 17 us -> 0.02 us  [local(): y_sum = lax.psum(y_part, 'rep') * (2.0 / math.sqrt(all_sources))]
    psum x1, waiting for transfers between devices: 145 us -> 136 us  [local(): z_gram = lax.psum(z_gram_part, ('pts', 'rep'))]
    all_to_all x0 -> x1, starting transfers between devices: none -> 9.61 us  [local(): pieces = lax.all_to_all(pieces, 'pts', split_axis=0, concat_axis=0)]
  transfers between devices with their start and end apart: 5 -> 5, of which waited for: 5 -> 2; matrix products, arithmetic and copies ran while one was open for 16% -> 23% of each run, Pallas kernels for 0% -> 0%
where the time goes in v1:
time: 710 us; the launch traced here: 707 us
  blocking collectives  270 us (38%)
  waiting for transfers between devices  240 us (34%)
  matrix products  148 us (21%)
  between operations  15.2 us (2%)
  other arithmetic  11.1 us (2%)
  local copies, waits for them, and re-layouts  10.2 us (1%)
  starting transfers between devices  9.77 us (1%)
    all_gather x1, blocking collectives, local(): src_all = lax.all_gather(source_xyz, 'pts', axis=1, tiled=True)  244 us
    psum x1, waiting for transfers between devices, local(): z_gram = lax.psum(z_gram_part, ('pts', 'rep'))  136 us
    psum x1, waiting for transfers between devices, local(): core_sum, y_gram = lax.psum((core_part, y_gram_part), 'pts')  104 us
    dot_general x32, matrix products, corange_inner(): lax.dot_general(tile, rows, (((0,), (0,)), ((), ())), preferred_element_t...  76.9 us
    dot_general x32, matrix products, range_inner(): jnp.dot(tile_block(target_xyz, where), rows, preferred_element_type=jnp.f...  65.2 us
    all_gather x1, blocking collectives, local(): tgt_all = lax.all_gather(target_xyz, 'pts', axis=1, tiled=True)  25.6 us
  transfers between devices with their start and end apart: 5, of which 2 were waited for; matrix products, arithmetic and copies ran while one was open for 23% of the time, Pallas kernels for 0%

profile of v1, /device:TPU:1, one launch (start us, length us, event | category | flops | bytes accessed | tf_op | source)
XLA Modules:
  0.0 706.7 jit_solution(6561683813296978070)
XLA Ops:
  11.6 6.0 stack.2
  17.6 9.6 %all-to-all-start = ((bf16[32,1024,256]{2,1,0:T(8,128)(2,1)}), bf16[32,1024,256]{2,1,0:T(8,128)(2,1)}, u32[]{:S(2)}, u32[]{:S(2)}) async-start(bf16[32,1024,256]{2,1,0:T(8,128)(2,1)} %stack.2), calls=%async_computation | async-start | bytes 33554432 | tf_op jit(solution)/shard_map/all_to_all | solution.py:49
  27.3 244.5 %all_gather.9 = f32[3,16384]{1,0:T(4,128)S(1)} all-gather(f32[3,512]{1,0:T(4,128)S(1)} %copy-done.4), channel_id=1, replica_groups=mesh['pts'=32,'rep'=4] {'pts'}, dimensions={1}, use_global_device_ids=true | all-gather | bytes 202752 | tf_op jit(solution)/shard_map/all_gather | solution.py:31
  271.8 25.6 %all_gather.11 = f32[3,32768]{1,0:T(4,128)S(1)} all-gather(f32[3,1024]{1,0:T(4,128)S(1)} %copy-done.3), channel_id=1, replica_groups=mesh['pts'=32,'rep'=4] {'pts'}, dimensions={1}, use_global_device_ids=true | all-gather | bytes 405504 | tf_op jit(solution)/shard_map/all_gather | solution.py:46
  297.4 69.5 %while.28 = (s32[]{:T(128)}, f32[1024,256]{1,0:T(8,128)S(1)}, f32[3,1024]{1,0:T(4,128)S(1)}, f32[3,16384]{1,0:T(4,128)S(1)}, bf16[16384,256]{1,0:T(8,128)(2,1)},...) while((s32[]{:T(128)}, f32[1024,256]{1,0:T(8,128)S(1)}, ...), condition=%wide.region_1.2_spmd.clone, body=%wide.region_0.1_spmd.clone.sunk | while | flops 274727424 | bytes 2414797 | solution.py:41
  299.7 2.0 convolution_add_fusion.4
  301.9 2.0 convolution_add_fusion.4
  304.1 2.0 convolution_add_fusion.4
  306.2 2.0 convolution_add_fusion.4
  308.4 2.0 convolution_add_fusion.4
  312.8 2.0 convolution_add_fusion.4
  314.9 2.0 convolution_add_fusion.4
  317.1 2.0 convolution_add_fusion.4
  319.3 2.0 convolution_add_fusion.4
  321.4 2.0 convolution_add_fusion.4
  327.9 2.0 convolution_add_fusion.4
  330.1 2.0 convolution_add_fusion.4
  332.3 2.0 convolution_add_fusion.4
  334.5 2.0 convolution_add_fusion.4
  341.0 2.0 convolution_add_fusion.4
  343.1 2.0 convolution_add_fusion.4
  345.3 2.0 convolution_add_fusion.4
  347.5 2.0 convolution_add_fusion.4
  354.0 2.0 convolution_add_fusion.4
  356.2 2.0 convolution_add_fusion.4
  358.3 2.0 convolution_add_fusion.4
  360.5 2.0 convolution_add_fusion.4
  364.9 2.0 convolution_add_fusion.4
  368.0 81.4 %while.29 = (s32[]{:T(128)}, f32[512,256]{1,0:T(8,128)S(1)}, f32[3,32768]{1,0:T(4,128)S(1)}, f32[3,512]{1,0:T(4,128)S(1)}, bf16[32768,256]{1,0:T(8,128)(2,1)}, /...) while((s32[]{:T(128)}, f32[512,256]{1,0:T(8,128)S(1)}, ...), condition=%wide.region_4.5_spmd.clone, body=%wide.region_3.4_spmd.clone.sunk | while | flops 274465280 | bytes 1628365 | solution.py:60
  368.1 2.4 convolution_add_fusion.5
  370.6 2.4 convolution_add_fusion.5
  373.2 2.4 convolution_add_fusion.5
  375.7 2.4 convolution_add_fusion.5
  378.3 2.4 convolution_add_fusion.5
  380.8 2.4 convolution_add_fusion.5
  383.4 2.4 convolution_add_fusion.5
  385.9 2.4 convolution_add_fusion.5
  388.5 2.4 convolution_add_fusion.5
  391.0 2.4 convolution_add_fusion.5
  393.5 2.4 convolution_add_fusion.5
  396.1 2.4 convolution_add_fusion.5
  398.6 2.4 convolution_add_fusion.5
  401.2 2.4 convolution_add_fusion.5
  403.7 2.4 convolution_add_fusion.5
  406.3 2.4 convolution_add_fusion.5
  408.8 2.4 convolution_add_fusion.5
  411.4 2.4 convolution_add_fusion.5
  413.9 2.4 convolution_add_fusion.5
  416.5 2.4 convolution_add_fusion.5
  419.0 2.4 convolution_add_fusion.5
  421.6 2.4 convolution_add_fusion.5
  424.1 2.4 convolution_add_fusion.5
  426.6 2.4 convolution_add_fusion.5
  429.2 2.4 convolution_add_fusion.5
  431.7 2.4 convolution_add_fusion.5
  434.3 2.4 convolution_add_fusion.5
  436.8 2.4 convolution_add_fusion.5
  439.4 2.4 convolution_add_fusion.5
  441.9 2.4 convolution_add_fusion.5
  444.4 2.4 convolution_add_fusion.5
  447.0 2.4 convolution_add_fusion.5
  452.8 2.5 fusion.22
  456.9 135.6 %all-reduce.7.cloned.1.call-done = f32[256,256]{1,0:T(8,128)} async-done(((f32[256,256]{1,0:T(8,128)}), f32[256,256]{1,0:T(8,128)}) %all-reduce.7.cloned.1.call-update) | async-done | bytes 262160 | tf_op jit(solution)/shard_map/psum | solution.py:69
  594.2 104.1 %all-reduce.9.cloned.1.call-done = (f32[256,256]{1,0:T(8,128)}, f32[256,256]{1,0:T(8,128)}) async-done(((f32[256,256]{1,0:T(8,128)}, f32[256,256]{1,0:T(8,128)}), (f32[256,256]{1,0:T(8,128)}, f32[256,256]{1,0:T(8,128)})) %all-reduce.9.cloned.1.call-update) | async-done | bytes 524304 | tf_op jit(solution)/shard_map/psum | solution.py:68
  (170 shorter events, 37.1 us)
Async XLA Ops:
  7.2 290.3 %all-gather.2.cloned.1.call-start = ((), (), s32[]{:S(2)}) async-start(), calls=%async_computation.1 | async-start | bytes 8650752 | tf_op jit(solution)/shard_map/all_gather | solution.py:32
  17.6 9.7 %copy-start.4 = (f32[3,512]{1,0:T(4,128)S(1)}, f32[3,512]{1,0:T(4,128)}, u32[]{:S(2)}) copy-start(f32[3,512]{1,0:T(4,128)} %param.11) | copy-start | bytes 18436
  17.6 254.2 %copy-start.3 = (f32[3,1024]{1,0:T(4,128)S(1)}, f32[3,1024]{1,0:T(4,128)}, u32[]{:S(2)}) copy-start(f32[3,1024]{1,0:T(4,128)} %param.10) | copy-start | bytes 36868
  17.6 350.4 %all-to-all-start = ((bf16[32,1024,256]{2,1,0:T(8,128)(2,1)}), bf16[32,1024,256]{2,1,0:T(8,128)(2,1)}, u32[]{:S(2)}, u32[]{:S(2)}) async-start(bf16[32,1024,256]{2,1,0:T(8,128)(2,1)} %stack.2), calls=%async_computation | async-start | bytes 33554432 | tf_op jit(solution)/shard_map/all_to_all | solution.py:49
  27.2 424.2 %all-reduce.5.cloned.1.call-start = ((), (), s32[]{:S(2)}) async-start(), calls=%async_computation.2 | async-start | bytes 2097152 | tf_op jit(solution)/shard_map/psum | solution.py:44
  366.9 1.0 copy-start.2
  367.9 224.6 %all-reduce.7.cloned.1.call-start = ((), (), s32[]{:S(2)}) async-start(), calls=%async_computation.3 | async-start | bytes 524288 | tf_op jit(solution)/shard_map/psum | solution.py:69
  449.5 5.8 copy-start.1
  451.3 247.0 %all-reduce.9.cloned.1.call-start = ((), (), s32[]{:S(2)}) async-start(), calls=%async_computation.4 | async-start | bytes 1048576 | tf_op jit(solution)/shard_map/psum | solution.py:68
  452.8 4.1 copy-start
Sparse Core Ops, SparseCore 0:
  10.8 210.5 all-gather.1
  368.0 42.2 all-reduce.4
  451.4 141.0 all-reduce.6
  596.2 102.0 all-reduce.8
